TPU v7x, 32 devices: a whole 2x2x4 slice. The times are simulated.
32 devices in a mesh: panel: 2 (over y), row: 4 (over z), layer: 4 (over x, core).
Axes of the slice: x: 2, y: 2, z: 4, core: 2. Of those that a mesh axis runs over, the one named last changes fastest.
Arguments:
- layers: bfloat16 [4, 8192, 512], P('layer', 'row', 'panel'), parts along dimension 2, may hold values from -6 to 6
- table: bfloat16 [16, 128, 64], replicated, may hold values from -0.375 to 0.375
- fitting: bfloat16 [8192, 6600], P('row', 'layer'), may hold values from -0.09375 to 0.09375
- owner: int32 [4, 128, 1], P('layer', 'row'), may hold values from 0 to 3; in each aligned block of 32 rows (0 to 31, 32 to 63, ..., all dimensions but the last counted through in order) at most 16 rows name the same one
- local_slice: int32 [4, 128], P('layer', 'row'), may hold values from 0 to 15
- block_index: int32 [4, 128], P('layer', 'row'), may hold values from 0 to 31
- weight_index: int32 [4, 128], P('layer', 'row'), may hold values from 0 to 15
Outputs:
- actuators: bfloat16 [512, 6600], P(('panel', 'row'), 'layer'), parts along dimension 0
There are 2 independent parts, one for each index of `panel`. A program takes and returns all parts, laid end to end along the dimension named above; an argument that names none is the same for every part. Nothing has to cross between parts.
Inputs may be any that keep to these rules, and one draw needn't show every extreme that they name: `owner`: within the 32 entries of one layer on one row device (aligned blocks of 32 entries), no value is named more than 16 times, and in every draw some block names one value exactly 16 times.
All inputs are finite; a program needn't handle non-finite values.
Results may differ from a plain program's by a relative error of at most 0.0058.
Values may be sent and summed in bfloat16 or wider, within the bound.
A program may use at most 64 MiB of HBM per device.

v0:
```python
import jax
import jax.numpy as jnp
from jax import lax
from jax.sharding import PartitionSpec as P


def local(layers, table, fitting, owner, local_slice, block_index, weight_index):
    rows_dev = layers.shape[1]
    columns = layers.shape[2]
    slice_rows = table.shape[1]
    block_rows = table.shape[2]
    entries = owner.shape[1]
    peer_count = lax.axis_size("row")
    capacity = max(2, 2 * entries // peer_count)
    slot_count = peer_count * capacity
    owned_slices = fitting.shape[0] // slice_rows
    owner_now = owner[0, :, 0]
    local_now = local_slice[0]
    owner_match = (owner_now[:, None] == jnp.arange(peer_count, dtype=jnp.int32)[None, :]).astype(
        jnp.int32
    )
    slot_rank = jnp.sum((jnp.cumsum(owner_match, axis=0) - 1) * owner_match, axis=1)
    target = owner_now * capacity + slot_rank
    placed = target[None, :] == jnp.arange(slot_count, dtype=jnp.int32)[:, None]
    filled = jnp.any(placed, axis=1)
    source = jnp.sum(jnp.where(placed, jnp.arange(entries, dtype=jnp.int32)[None, :], 0), axis=1)
    send_local = jnp.where(filled, local_now[source], -1).reshape(peer_count, capacity)
    grouped = layers[0].reshape(rows_dev // block_rows, block_rows, columns)
    picked = grouped[block_index[0][source]].reshape(peer_count, capacity, block_rows, columns)
    send_weight = weight_index[0][source].reshape(peer_count, capacity)
    got_rows, got_weight, got_local = (
        lax.all_to_all(picked, "row", split_axis=0, concat_axis=0, tiled=True),
        lax.all_to_all(send_weight, "row", split_axis=0, concat_axis=0, tiled=True),
        lax.all_to_all(send_local, "row", split_axis=0, concat_axis=0, tiled=True),
    )
    pupil_terms = jnp.einsum(
        "ksb,kbc->ksc",
        table[got_weight.reshape(-1)],
        got_rows.reshape(slot_count, block_rows, columns),
        preferred_element_type=jnp.float32,
    ).astype(jnp.bfloat16)
    selector = (
        jnp.arange(owned_slices, dtype=jnp.int32)[:, None] == got_local.reshape(-1)[None, :]
    ).astype(jnp.bfloat16)
    partial_pupil = jnp.dot(
        selector,
        pupil_terms.reshape(slot_count, slice_rows * columns),
        preferred_element_type=jnp.float32,
    ).reshape(owned_slices * slice_rows, columns)
    pupil_rounded = lax.psum(partial_pupil, "layer").astype(jnp.bfloat16)
    return lax.psum_scatter(
        lax.dot_general(
            pupil_rounded, fitting, (((0,), (0,)), ((), ())), preferred_element_type=jnp.float32
        ),
        "row",
        scatter_dimension=0,
        tiled=True,
    ).astype(jnp.bfloat16)


def solution(mesh):
    return jax.shard_map(
        local,
        mesh=mesh,
        in_specs=(
            P("layer", "row", "panel"),
            P(),
            P("row", "layer"),
            P("layer", "row", None),
            P("layer", "row"),
            P("layer", "row"),
            P("layer", "row"),
        ),
        out_specs=P(("panel", "row"), "layer"),
        check_vma=False,
    )
```

profile of v0, /device:TPU:0, one launch (start us, length us, event | category | flops | bytes accessed | tf_op | source)
XLA Modules:
  0.0 183.3 jit_solution(12246338649943333909)
XLA Ops:
  6.5 0.0 copy-start
  6.5 0.8 fusion.3
  7.4 0.1 reduce_window_sum.11
  7.4 0.8 select_reduce_fusion.1
  8.2 0.7 multiply_add_fusion
  8.9 0.1 select_reduce_fusion
  9.0 1.4 gather_fusion.1
  10.4 0.7 all_to_all.14
  11.1 6.3 %all-to-all-start.1 = ((s32[4,1,16]{2,1,0:T(1,128)}), s32[4,1,16]{2,1,0:T(1,128)S(1)}, u32[]{:S(2)}, u32[]{:S(2)}) async-start(s32[4,1,16]{2,1,0:T(1,128)} %bitcast.6), calls=%async_computation.1 | async-start | bytes 4096 | tf_op jit(solution)/shard_map/all_to_all | solution.py:33
  17.5 0.1 fusion.2
  17.6 1.4 gather_fusion.3
  19.0 1.4 gather_fusion
  20.4 0.7 select_n.54
  21.1 1.8 %all-to-all-done.1 = s32[4,1,16]{2,1,0:T(1,128)S(1)} async-done(((s32[4,1,16]{2,1,0:T(1,128)}), s32[4,1,16]{2,1,0:T(1,128)S(1)}, u32[]{:S(2)}, u32[]{:S(2)}) %all-to-all-start.1) | async-done | bytes 288 | tf_op jit(solution)/shard_map/all_to_all | solution.py:33
  23.0 3.2 %all-to-all-start = ((s32[4,1,16]{2,1,0:T(1,128)}), s32[4,1,16]{2,1,0:T(1,128)S(1)}, u32[]{:S(2)}, u32[]{:S(2)}) async-start(s32[4,1,16]{2,1,0:T(1,128)} %bitcast.4), calls=%async_computation | async-start | bytes 4096 | tf_op jit(solution)/shard_map/all_to_all | solution.py:34
  26.2 0.0 copy-done
  26.2 2.0 %gather_fusion.4 = bf16[64,64,256]{2,1,0:T(8,128)(2,1)} fusion(bf16[32,64,256]{2,1,0:T(8,128)(2,1)S(1)} %bitcast.27, s32[1024]{0:T(1024)S(1)} %pad_clamp_fusion), kind=kCustom, calls=%fused_computation.4 | custom fusion | bytes 4194560 | tf_op jit(solution)/shard_map/gather | solution.py:29
  28.3 3.5 %all-to-all-done = s32[4,1,16]{2,1,0:T(1,128)S(1)} async-done(((s32[4,1,16]{2,1,0:T(1,128)}), s32[4,1,16]{2,1,0:T(1,128)S(1)}, u32[]{:S(2)}, u32[]{:S(2)}) %all-to-all-start) | async-done | bytes 288 | tf_op jit(solution)/shard_map/all_to_all | solution.py:34
  31.8 0.0 copy-start.1
  31.8 4.6 %all-to-all-start.2 = ((bf16[4,16,64,256]{3,2,1,0:T(8,128)(2,1)}), bf16[4,16,64,256]{3,2,1,0:T(8,128)(2,1)}, u32[]{:S(2)}, u32[]{:S(2)}) async-start(bf16[4,16,64,256]{3,2,1,0:T(8,128)(2,1)} %bitcast.12), calls=%async_computation.2 | async-start | bytes 4194304 | tf_op jit(solution)/shard_map/all_to_all | solution.py:32
  36.4 0.0 reduce-scatter.2.cloned.1.call-start
  36.4 0.5 broadcast.101
  36.9 0.7 reduce.6
  37.6 0.1 reshape.109
  37.7 0.7 reduce.7
  38.4 0.1 eq.48
  38.5 0.0 copy-done.1
  38.5 0.7 gather_fusion.2
  39.2 43.5 %all-to-all-done.2 = bf16[4,16,64,256]{3,2,1,0:T(8,128)(2,1)} async-done(((bf16[4,16,64,256]{3,2,1,0:T(8,128)(2,1)}), bf16[4,16,64,256]{3,2,1,0:T(8,128)(2,1)}, u32[]{:S(2)}, u32[]{:S(2)}) %all-to-all-start.2) | async-done | bytes 2097184 | tf_op jit(solution)/shard_map/all_to_all | solution.py:32
  82.8 2.9 %convolution_convert_fusion = bf16[64,128,256]{2,1,0:T(8,128)(2,1)S(1)} fusion(bf16[64,128,64]{1,2,0:T(8,128)(2,1)S(1)} %gather_fusion.2, bf16[64,64,256]{2,1,0:T(8,128)(2,1)} %bitcast.13), kind=kOutput, calls=%fused_computation.5 | convolution fusion | flops 270532608 | bytes 7340032 | tf_op jit(solution)/shard_map/ksb,kbc->ksc/dot_general | solution.py:36
  85.7 2.6 %copy.12 = bf16[8,8,128,256]{3,1,2,0:T(8,128)(2,1)S(1)} copy(bf16[8,8,128,256]{3,2,1,0:T(8,128)(2,1)S(1)} %bitcast.31) | data formatting | bytes 8388608
  88.3 0.7 fusion.4
  89.0 1.5 reshape.113
  90.5 40.8 %all-reduce.1 = bf16[2048,256]{1,0:T(8,128)(2,1)S(1)} all-reduce(f32[2048,256]{1,0:T(8,128)} %reshape.113), channel_id=1, replica_groups=mesh['panel'=2,'row'=4,'layer'=4] {'layer'}, use_global_device_ids=true, to_apply=%region_4.5 | all-reduce | flops 524288 | bytes 3145728 | tf_op jit(solution)/shard_map/psum | solution.py:50
  131.3 6.2 %fusion.9 = f32[256,1650]{1,0:T(8,128)} fusion(bf16[2048,256]{1,0:T(8,128)(2,1)S(1)} %all-reduce.1, bf16[2048,1650]{0,1:T(8,128)(2,1)} %param.9), kind=kOutput, calls=%fused_computation.28 | convolution fusion | flops 1730150400 | bytes 9496576 | tf_op jit(solution)/shard_map/dot_general | solution.py:52
  137.5 0.0 reduce-scatter.2.cloned.1.call-update
  137.5 37.2 %reduce-scatter.2.cloned.1.call-done = f32[64,1650]{1,0:T(8,128)} async-done(((f32[256,1650]{1,0:T(8,128)}), f32[64,1650]{1,0:T(8,128)}) %reduce-scatter.2.cloned.1.call-update) | async-done | bytes 422416 | tf_op jit(solution)/shard_map/reduce_scatter | solution.py:51
  174.7 1.7 convert_element_type.16
  (7 shorter events, 0.0 us)
Async XLA Ops:
  6.5 19.7 %copy-start = (bf16[1,2048,256]{2,1,0:T(8,128)(2,1)S(1)}, bf16[1,2048,256]{2,1,0:T(8,128)(2,1)}, u32[]{:S(2)}) copy-start(bf16[1,2048,256]{2,1,0:T(8,128)(2,1)} %param.7) | copy-start | bytes 3145732
  11.1 11.8 %all-to-all-start.1 = ((s32[4,1,16]{2,1,0:T(1,128)}), s32[4,1,16]{2,1,0:T(1,128)S(1)}, u32[]{:S(2)}, u32[]{:S(2)}) async-start(s32[4,1,16]{2,1,0:T(1,128)} %bitcast.6), calls=%async_computation.1 | async-start | bytes 4096 | tf_op jit(solution)/shard_map/all_to_all | solution.py:33
  23.0 8.8 %all-to-all-start = ((s32[4,1,16]{2,1,0:T(1,128)}), s32[4,1,16]{2,1,0:T(1,128)S(1)}, u32[]{:S(2)}, u32[]{:S(2)}) async-start(s32[4,1,16]{2,1,0:T(1,128)} %bitcast.4), calls=%async_computation | async-start | bytes 4096 | tf_op jit(solution)/shard_map/all_to_all | solution.py:34
  31.8 6.7 %copy-start.1 = (bf16[16,128,64]{1,2,0:T(8,128)(2,1)S(1)}, bf16[16,128,64]{1,2,0:T(8,128)(2,1)}, u32[]{:S(2)}) copy-start(bf16[16,128,64]{1,2,0:T(8,128)(2,1)} %param.8) | copy-start | bytes 786436
  31.8 51.0 %all-to-all-start.2 = ((bf16[4,16,64,256]{3,2,1,0:T(8,128)(2,1)}), bf16[4,16,64,256]{3,2,1,0:T(8,128)(2,1)}, u32[]{:S(2)}, u32[]{:S(2)}) async-start(bf16[4,16,64,256]{3,2,1,0:T(8,128)(2,1)} %bitcast.12), calls=%async_computation.2 | async-start | bytes 4194304 | tf_op jit(solution)/shard_map/all_to_all | solution.py:32
  36.4 138.4 %reduce-scatter.2.cloned.1.call-start = ((), (), s32[]{:S(2)}) async-start(), calls=%async_computation.4 | async-start | bytes 2129920 | tf_op jit(solution)/shard_map/reduce_scatter | solution.py:51
Sparse Core Ops, SparseCore 0:
  137.7 37.0 reduce-scatter.1
where the time goes:
time: 184 us; the launch traced here: 183 us
  waiting for transfers between devices  86.1 us (47%)
  blocking collectives  40.8 us (22%)
  starting transfers between devices  14.2 us (8%)
  between operations  13.5 us (7%)
  local copies, waits for them, and re-layouts  13.2 us (7%)
  matrix products  9.8 us (5%)
  other arithmetic  5.64 us (3%)
    all_to_all x1, waiting for transfers between devices, local(): lax.all_to_all(picked, 'row', split_axis=0, concat_axis=0, tiled=True)  43.5 us
    psum x1, blocking collectives, local(): pupil_rounded = lax.psum(partial_pupil, 'layer').astype(jnp.bfloat16)  40.8 us
    reduce_scatter x1, waiting for transfers between devices, local(): lax.psum_scatter(lax.dot_general(pupil_rounded, fitting, (((0,), (0,)), (...  37.2 us
    all_to_all x1, starting transfers between devices, local(): lax.all_to_all(send_weight, 'row', split_axis=0, concat_axis=0, tiled=True)  6.35 us
    dot_general x1, matrix products, local(): lax.dot_general(pupil_rounded, fitting, (((0,), (0,)), ((), ())), preferr...  6.23 us
    all_to_all x1, starting transfers between devices, local(): lax.all_to_all(picked, 'row', split_axis=0, concat_axis=0, tiled=True)  4.58 us
  transfers between devices with their start and end apart: 4, of which 4 were waited for; matrix products, arithmetic and copies ran while one was open for 5% of the time, Pallas kernels for 0%

commit v1 on v0

--- a/solution.py
+++ b/solution.py
@@ -47,7 +47,7 @@
         pupil_terms.reshape(slot_count, slice_rows * columns),
         preferred_element_type=jnp.float32,
     ).reshape(owned_slices * slice_rows, columns)
-    pupil_rounded = lax.psum(partial_pupil, "layer").astype(jnp.bfloat16)
+    pupil_rounded = jnp.sum(lax.all_gather(partial_pupil, "layer"), axis=0).astype(jnp.bfloat16)
     return lax.psum_scatter(
         lax.dot_general(
             pupil_rounded, fitting, (((0,), (0,)), ((), ())), preferred_element_type=jnp.float32

time: 184 us -> 205 us (1.11)
  waiting for transfers between devices: 86.1 us -> 144 us
  blocking collectives: 40.8 us -> 0 us
  other arithmetic: 5.64 us -> 9.88 us
    all_gather x0 -> x1, waiting for transfers between devices: none -> 57.5 us  [local(): lax.all_gather(partial_pupil, 'layer')]
    psum x1 -> x0, blocking collectives: 40.8 us -> none  [local(): pupil_rounded = lax.psum(partial_pupil, 'layer').astype(jnp.bfloat16)]
    reduce_sum x0 -> x1, other arithmetic: none -> 4.25 us  [local(): jnp.sum(lax.all_gather(partial_pupil, 'layer'), axis=0).astype(jnp.bfloat16)]
  transfers between devices with their start and end apart: 4 -> 5, of which waited for: 4 -> 5; matrix products, arithmetic and copies ran while one was open for 5% -> 4% of each run, Pallas kernels for 0% -> 0%
where the time goes in v1:
time: 205 us
  waiting for transfers between devices  144 us (70%)
  starting transfers between devices  14.3 us (7%)
  between operations  13.5 us (7%)
  local copies, waits for them, and re-layouts  13.3 us (6%)
  other arithmetic  9.88 us (5%)
  matrix products  9.81 us (5%)
    all_gather x1, waiting for transfers between devices, local(): lax.all_gather(partial_pupil, 'layer')  57.5 us
    all_to_all x1, waiting for transfers between devices, local(): lax.all_to_all(picked, 'row', split_axis=0, concat_axis=0, tiled=True)  43.5 us
    reduce_scatter x1, waiting for transfers between devices, local(): lax.psum_scatter(lax.dot_general(pupil_rounded, fitting, (((0,), (0,)), (...  37.6 us
    all_to_all x1, starting transfers between devices, local(): lax.all_to_all(send_weight, 'row', split_axis=0, concat_axis=0, tiled=True)  6.35 us
    dot_general x1, matrix products, local(): lax.dot_general(pupil_rounded, fitting, (((0,), (0,)), ((), ())), preferr...  6.24 us
    all_to_all x1, starting transfers between devices, local(): lax.all_to_all(picked, 'row', split_axis=0, concat_axis=0, tiled=True)  4.58 us
    reduce_sum x1, other arithmetic, local(): jnp.sum(lax.all_gather(partial_pupil, 'layer'), axis=0).astype(jnp.bfloat16)  4.25 us
  transfers between devices with their start and end apart: 5, of which 5 were waited for; matrix products, arithmetic and copies ran while one was open for 4% of the time, Pallas kernels for 0%

profile of v1, /device:TPU:0, one launch (start us, length us, event | category | flops | bytes accessed | tf_op | source)
XLA Modules:
  0.0 204.8 jit_solution(18249702565941611050)
XLA Ops:
  6.5 0.0 copy-start
  6.5 0.8 fusion.3
  7.4 0.1 reduce_window_sum.11
  7.4 0.8 select_reduce_fusion.1
  8.2 0.7 multiply_add_fusion
  8.9 0.1 select_reduce_fusion
  9.0 1.4 gather_fusion.1
  10.4 0.7 all_to_all.14
  11.1 6.3 %all-to-all-start.1 = ((s32[4,1,16]{2,1,0:T(1,128)}), s32[4,1,16]{2,1,0:T(1,128)S(1)}, u32[]{:S(2)}, u32[]{:S(2)}) async-start(s32[4,1,16]{2,1,0:T(1,128)} %bitcast.6), calls=%async_computation.1 | async-start | bytes 4096 | tf_op jit(solution)/shard_map/all_to_all | solution.py:33
  17.5 0.1 fusion.2
  17.6 1.4 gather_fusion.3
  19.0 1.4 gather_fusion
  20.4 0.7 select_n.54
  21.1 1.8 all-to-all-done.1
  23.0 3.2 %all-to-all-start = ((s32[4,1,16]{2,1,0:T(1,128)}), s32[4,1,16]{2,1,0:T(1,128)S(1)}, u32[]{:S(2)}, u32[]{:S(2)}) async-start(s32[4,1,16]{2,1,0:T(1,128)} %bitcast.4), calls=%async_computation | async-start | bytes 4096 | tf_op jit(solution)/shard_map/all_to_all | solution.py:34
  26.2 0.0 copy-done
  26.2 2.0 gather_fusion.4
  28.3 3.5 %all-to-all-done = s32[4,1,16]{2,1,0:T(1,128)S(1)} async-done(((s32[4,1,16]{2,1,0:T(1,128)}), s32[4,1,16]{2,1,0:T(1,128)S(1)}, u32[]{:S(2)}, u32[]{:S(2)}) %all-to-all-start) | async-done | bytes 288 | tf_op jit(solution)/shard_map/all_to_all | solution.py:34
  31.8 0.0 copy-start.1
  31.8 4.6 %all-to-all-start.2 = ((bf16[4,16,64,256]{3,2,1,0:T(8,128)(2,1)}), bf16[4,16,64,256]{3,2,1,0:T(8,128)(2,1)}, u32[]{:S(2)}, u32[]{:S(2)}) async-start(bf16[4,16,64,256]{3,2,1,0:T(8,128)(2,1)} %bitcast.12), calls=%async_computation.2 | async-start | bytes 4194304 | tf_op jit(solution)/shard_map/all_to_all | solution.py:32
  36.4 0.0 all-gather.2.cloned.1.call-start
  36.4 0.5 broadcast.101
  36.9 0.7 reduce.6
  37.6 0.1 reshape.106
  37.7 0.7 reduce.7
  38.4 0.1 eq.48
  38.5 0.0 copy-done.1
  38.5 0.7 gather_fusion.2
  39.2 43.5 %all-to-all-done.2 = bf16[4,16,64,256]{3,2,1,0:T(8,128)(2,1)} async-done(((bf16[4,16,64,256]{3,2,1,0:T(8,128)(2,1)}), bf16[4,16,64,256]{3,2,1,0:T(8,128)(2,1)}, u32[]{:S(2)}, u32[]{:S(2)}) %all-to-all-start.2) | async-done | bytes 2097184 | tf_op jit(solution)/shard_map/all_to_all | solution.py:32
  82.8 2.9 %convolution_convert_fusion = bf16[64,128,256]{2,1,0:T(8,128)(2,1)S(1)} fusion(bf16[64,128,64]{1,2,0:T(8,128)(2,1)S(1)} %gather_fusion.2, bf16[64,64,256]{2,1,0:T(8,128)(2,1)} %bitcast.13), kind=kOutput, calls=%fused_computation.5 | convolution fusion | flops 270532608 | bytes 7340032 | tf_op jit(solution)/shard_map/ksb,kbc->ksc/dot_general | solution.py:36
  85.7 2.6 %copy.12 = bf16[8,8,128,256]{3,1,2,0:T(8,128)(2,1)S(1)} copy(bf16[8,8,128,256]{3,2,1,0:T(8,128)(2,1)S(1)} %bitcast.31) | data formatting | bytes 8388608
  88.3 0.7 fusion.4
  89.0 1.6 all_gather_reshape.3
  90.5 0.0 all-gather.2.cloned.1.call-update
  90.5 0.0 reduce-scatter.2.cloned.1.call-start
  90.6 57.5 %all-gather.2.cloned.1.call-done = f32[4,2048,256]{2,1,0:T(8,128)} async-done(((f32[1,2048,256]{2,1,0:T(8,128)}), f32[4,2048,256]{2,1,0:T(8,128)}) %all-gather.2.cloned.1.call-update) | async-done | bytes 8388624 | tf_op jit(solution)/shard_map/all_gather | solution.py:50
  148.1 4.2 %reduce_sum.32 = bf16[2048,256]{1,0:T(8,128)(2,1)S(1)} reduce(f32[4,2048,256]{2,1,0:T(8,128)} %all-gather.2.cloned.1.call-done, f32[]{:T(128)} %constant.5.clone.1), dimensions={0}, to_apply=%region_4.5 | reduce | flops 1572864 | bytes 9437188 | tf_op jit(solution)/shard_map/reduce_sum | solution.py:50
  152.3 6.2 %fusion.9 = f32[256,1650]{1,0:T(8,128)} fusion(bf16[2048,256]{1,0:T(8,128)(2,1)S(1)} %reduce_sum.32, bf16[2048,1650]{0,1:T(8,128)(2,1)} %param.9), kind=kOutput, calls=%fused_computation.28 | convolution fusion | flops 1730150400 | bytes 9496576 | tf_op jit(solution)/shard_map/dot_general | solution.py:52
  158.6 0.0 reduce-scatter.2.cloned.1.call-update
  158.6 37.6 %reduce-scatter.2.cloned.1.call-done = f32[64,1650]{1,0:T(8,128)} async-done(((f32[256,1650]{1,0:T(8,128)}), f32[64,1650]{1,0:T(8,128)}) %reduce-scatter.2.cloned.1.call-update) | async-done | bytes 422416 | tf_op jit(solution)/shard_map/reduce_scatter | solution.py:51
  196.2 1.7 convert_element_type.16
  (7 shorter events, 0.0 us)
Async XLA Ops:
  6.5 19.7 %copy-start = (bf16[1,2048,256]{2,1,0:T(8,128)(2,1)S(1)}, bf16[1,2048,256]{2,1,0:T(8,128)(2,1)}, u32[]{:S(2)}) copy-start(bf16[1,2048,256]{2,1,0:T(8,128)(2,1)} %param.7) | copy-start | bytes 3145732
  11.1 11.8 %all-to-all-start.1 = ((s32[4,1,16]{2,1,0:T(1,128)}), s32[4,1,16]{2,1,0:T(1,128)S(1)}, u32[]{:S(2)}, u32[]{:S(2)}) async-start(s32[4,1,16]{2,1,0:T(1,128)} %bitcast.6), calls=%async_computation.1 | async-start | bytes 4096 | tf_op jit(solution)/shard_map/all_to_all | solution.py:33
  23.0 8.8 %all-to-all-start = ((s32[4,1,16]{2,1,0:T(1,128)}), s32[4,1,16]{2,1,0:T(1,128)S(1)}, u32[]{:S(2)}, u32[]{:S(2)}) async-start(s32[4,1,16]{2,1,0:T(1,128)} %bitcast.4), calls=%async_computation | async-start | bytes 4096 | tf_op jit(solution)/shard_map/all_to_all | solution.py:34
  31.8 6.7 %copy-start.1 = (bf16[16,128,64]{1,2,0:T(8,128)(2,1)S(1)}, bf16[16,128,64]{1,2,0:T(8,128)(2,1)}, u32[]{:S(2)}) copy-start(bf16[16,128,64]{1,2,0:T(8,128)(2,1)} %param.8) | copy-start | bytes 786436
  31.8 51.0 %all-to-all-start.2 = ((bf16[4,16,64,256]{3,2,1,0:T(8,128)(2,1)}), bf16[4,16,64,256]{3,2,1,0:T(8,128)(2,1)}, u32[]{:S(2)}, u32[]{:S(2)}) async-start(bf16[4,16,64,256]{3,2,1,0:T(8,128)(2,1)} %bitcast.12), calls=%async_computation.2 | async-start | bytes 4194304 | tf_op jit(solution)/shard_map/all_to_all | solution.py:32
  36.4 111.7 %all-gather.2.cloned.1.call-start = ((), (), s32[]{:S(2)}) async-start(), calls=%async_computation.4 | async-start | bytes 10485760 | tf_op jit(solution)/shard_map/all_gather | solution.py:50
  90.5 105.7 %reduce-scatter.2.cloned.1.call-start = ((), (), s32[]{:S(2)}) async-start(), calls=%async_computation.5 | async-start | bytes 2129920 | tf_op jit(solution)/shard_map/reduce_scatter | solution.py:51
Sparse Core Ops, SparseCore 0:
  90.7 57.3 all-gather.1
  158.7 37.4 reduce-scatter.1
